TPU v7x, 256 devices: a whole 4x4x8 slice. The times are simulated.
256 devices in a mesh: tm: 16 (over x, y), pairs: 16 (over z, core).
Axes of the slice: x: 4, y: 4, z: 8, core: 2. Of those that a mesh axis runs over, the one named last changes fastest.
Arguments:
- panels: bfloat16 [48, 16, 1024, 128], P('tm', None, 'pairs')
- pair_list: int32 [2, 262144], P(None, ('tm', 'pairs')), may hold values from 0 to 16383, as said below
- pair_count: int32 [256], P(('tm', 'pairs')), may hold values from 1 to 1024, as said below
Outputs:
- stacks: float32 [262144, 512], P(('tm', 'pairs'))
Inputs may be any that keep to these rules, and one draw needn't show every extreme that they name: `pair_list`: slots o * 1024 to (o + 1) * 1024 - 1 belong to owner o. The first channel of each is one of channels o * 64 to (o + 1) * 64 - 1; the second lies 1 to 100 channels after it, in the same section of 1024 channels. A distance of 100 occurs in every draw. Owner o's live slots are its first pair_count[o]. Some owner has all 1024 live in every draw.
All inputs are finite; a program needn't handle non-finite values.
Results may differ from a plain program's by a relative error of at most 0.015.
Values may be sent and summed in bfloat16 or wider, within the bound.
No kernel may reach another device: no remote copies, remote signals or barrier semaphores. Data moves between devices by JAX's collectives and lax.ppermute only.
A program may use at most 128 MiB of HBM per device.

v0:
```python
import math

import jax
import jax.numpy as jnp
from jax import lax
from jax.sharding import PartitionSpec as P

NB = 100
SEG = 512
SEGS = 12
TILE = 128
PAIR_BLOCK = 512


def from_behind(block, axis, distance):
    devices = range(lax.axis_size(axis))
    route = [(i - distance, i) for i in devices if i - distance in devices]
    return lax.ppermute(block, axis, route)


def phase_angles(left_index, right_index):
    phase_step = left_index * right_index % (2 * SEG)
    return phase_step.astype(jnp.float32) * (math.pi / SEG)


def split_table(table):
    table_high = table.astype(jnp.bfloat16)
    table_low = (table - table_high.astype(jnp.float32)).astype(jnp.bfloat16)
    return (table_high, table_low)


def forward_tables():
    sample_ids = jnp.arange(SEG, dtype=jnp.int32)[:, None]
    bin_ids = jnp.arange(SEG, dtype=jnp.int32)[None, :]
    angles = phase_angles(sample_ids, bin_ids)
    table = jnp.concatenate([jnp.cos(angles), -jnp.sin(angles)], axis=1) / math.sqrt(SEG)
    table_high, table_low = split_table(table)
    per_seg = SEG // TILE
    return (table_high.reshape(per_seg, TILE, 2 * SEG), table_low.reshape(per_seg, TILE, 2 * SEG))


def inverse_tables():
    bin_ids = jnp.arange(SEG, dtype=jnp.int32)[:, None]
    lag_ids = jnp.arange(SEG, dtype=jnp.int32)[None, :] - SEG // 2
    angles = phase_angles(bin_ids, lag_ids)
    weights = jnp.where(bin_ids == 0, 1.0, 2.0).astype(jnp.float32) / math.sqrt(SEG)
    table = jnp.concatenate([weights * jnp.cos(angles), -weights * jnp.sin(angles)], axis=0)
    return split_table(table)


def whiten(panel_rows, table_high, table_low):
    tile_count, channels, tile_width = panel_rows.shape
    grouped = panel_rows.reshape(SEGS, tile_count // SEGS, channels, tile_width)
    values = grouped.astype(jnp.float32)
    mean_square = jnp.mean(values * values, axis=(1, 3), keepdims=True)
    scaled = (values * lax.rsqrt(mean_square + 1e-05)).astype(jnp.bfloat16)
    spectrum = jnp.einsum("sqct,qtf->csf", scaled, table_high, preferred_element_type=jnp.float32)
    spectrum = spectrum + jnp.einsum(
        "sqct,qtf->csf", scaled, table_low, preferred_element_type=jnp.float32
    )
    bin_count = spectrum.shape[2] // 2
    real_part = spectrum[:, :, :bin_count]
    imag_part = spectrum[:, :, bin_count:]
    level_power = jnp.mean(real_part * real_part + imag_part * imag_part, axis=1, keepdims=True)
    weight_gain = lax.rsqrt(level_power + 0.5)
    return (spectrum * jnp.concatenate([weight_gain, weight_gain], axis=2)).astype(jnp.bfloat16)


def correlate(spectra, firsts, seconds, inv_high, inv_low):
    bin_count = spectra.shape[2] // 2
    segment_total = spectra.shape[1]
    left_rows = jnp.take(spectra, firsts, axis=0)
    right_rows = jnp.take(spectra, seconds, axis=0)
    left_real = left_rows[:, :, :bin_count]
    left_imag = left_rows[:, :, bin_count:]
    right_real = right_rows[:, :, :bin_count]
    right_imag = right_rows[:, :, bin_count:]
    real_sum = jnp.einsum("psk,psk->pk", left_real, right_real, preferred_element_type=jnp.float32)
    real_sum = real_sum + jnp.einsum(
        "psk,psk->pk", left_imag, right_imag, preferred_element_type=jnp.float32
    )
    imag_sum = jnp.einsum("psk,psk->pk", left_imag, right_real, preferred_element_type=jnp.float32)
    imag_sum = imag_sum - jnp.einsum(
        "psk,psk->pk", left_real, right_imag, preferred_element_type=jnp.float32
    )
    cross_spec = (jnp.concatenate([real_sum, imag_sum], axis=1) / segment_total).astype(
        jnp.bfloat16
    )
    lagged = jnp.dot(cross_spec, inv_high, preferred_element_type=jnp.float32)
    return lagged + jnp.dot(cross_spec, inv_low, preferred_element_type=jnp.float32)


def per_device(panels, pair_list, pair_count):
    relaid = lax.all_to_all(panels, "tm", split_axis=1, concat_axis=0, tiled=True)
    own_rows = relaid[:, 0]
    channels = own_rows.shape[1]
    reach_count = (NB + channels - 1) // channels
    fwd_high, fwd_low = forward_tables()
    inv_high, inv_low = inverse_tables()
    own_spec = whiten(own_rows, fwd_high, fwd_low)
    pieces_all = [own_spec]
    for distance in range(1, reach_count + 1):
        pieces_all.append(from_behind(own_spec, "pairs", -distance))
    spectra = jnp.concatenate(pieces_all, axis=0)
    offset = (lax.axis_index("tm") * lax.axis_size("pairs") + lax.axis_index("pairs")) * channels
    firsts = pair_list[0] - offset
    seconds = pair_list[1] - offset
    capacity = firsts.shape[0]
    live_count = pair_count[0]
    block_total = capacity // PAIR_BLOCK

    def one_block(pair_block):
        return correlate(spectra, pair_block[0], pair_block[1], inv_high, inv_low)

    results = lax.map(
        one_block,
        (firsts.reshape(block_total, PAIR_BLOCK), seconds.reshape(block_total, PAIR_BLOCK)),
    )
    stacks = results.reshape(capacity, SEG)
    live_mask = jnp.arange(capacity, dtype=jnp.int32) < live_count
    return jnp.where(live_mask[:, None], stacks, 0.0)


def solution(mesh):
    return jax.shard_map(
        per_device,
        mesh=mesh,
        in_specs=(P("tm", None, "pairs", None), P(None, ("tm", "pairs")), P(("tm", "pairs"))),
        out_specs=P(("tm", "pairs"), None),
        check_vma=False,
    )
```

profile of v0, /device:TPU:96, one launch (start us, length us, event | category | flops | bytes accessed | tf_op | source)
XLA Modules:
  0.0 283.5 jit_solution(17435599186772269249)
XLA Ops:
  0.0 2.1 copy.5
  2.1 7.0 %all-to-all-start = ((bf16[3,16,64,128]{3,2,0,1:T(8,128)(2,1)}), bf16[3,16,64,128]{3,2,0,1:T(8,128)(2,1)S(1)}, u32[]{:S(2)}, u32[]{:S(2)}) async-start(bf16[3,16,64,128]{3,2,0,1:T(8,128)(2,1)} %copy.5), calls=%async_computation | async-start | bytes 1572864 | tf_op jit(solution)/shard_map/all_to_all | solution.py:94
  9.1 4.2 %fusion.36 = (f32[4,128,512]{2,1,0:T(8,128)S(1)}, f32[4,128,512]{2,1,0:T(8,128)S(1)}) fusion(s32[4,128]{1,0:T(4,128)S(1)} %multiply_add_fusion), kind=kLoop, calls=%fused_computation.76 | loop fusion | flops 3932160 | bytes 2099200 | tf_op jit(solution)/shard_map/cos | solution.py:36
  13.3 10.1 %all-to-all-done = bf16[3,16,64,128]{3,2,0,1:T(8,128)(2,1)S(1)} async-done(((bf16[3,16,64,128]{3,2,0,1:T(8,128)(2,1)}), bf16[3,16,64,128]{3,2,0,1:T(8,128)(2,1)S(1)}, u32[]{:S(2)}, u32[]{:S(2)}) %all-to-all-start) | async-done | bytes 786464 | tf_op jit(solution)/shard_map/all_to_all | solution.py:94
  23.5 0.5 multiply_reduce_fusion
  24.1 0.2 convert_element_type.77
  24.2 1.0 fusion.20
  25.3 1.1 fusion.14
  26.4 0.4 fusion.18
  26.8 0.0 copy-start.2
  26.8 0.5 multiply_convert_fusion
  27.3 1.9 collective-permute-start
  29.2 2.2 collective-permute-start.1
  31.5 0.0 copy-done.2
  32.2 0.6 iota_compare_fusion
  32.8 4.2 %cosine_multiply_fusion = (f32[512,512]{1,0:T(8,128)S(1)}, f32[512,512]{1,0:T(8,128)S(1)}) fusion(s32[512]{0:T(512)S(1)} %iota_add_fusion, f32[512]{0:T(512)S(1)} %get-tuple-element.84, f32[512]{0:T(512)S(1)} %get-tuple-element.85), kind=kLoop, calls=%fused_computation.67 | loop fusion | flops 4194304 | bytes 2103296 | tf_op jit(solution)/shard_map/mul | solution.py:47
  37.0 1.1 fusion.15
  38.1 0.3 subtract_convert_fusion
  38.4 23.8 %collective-permute-done = bf16[64,12,1024]{2,0,1:T(8,128)(2,1)} collective-permute-done((bf16[64,12,1024]{2,0,1:T(8,128)(2,1)S(1)}, bf16[64,12,1024]{2,0,1:T(8,128)(2,1)}, u32[]{:S(2)}, u32[]{:S(2)}) %collective-permute-start) | collective-permute-done | bytes 1572896 | tf_op jit(solution)/shard_map/ppermute | solution.py:18
  62.2 22.3 %collective-permute-done.1 = bf16[64,12,1024]{2,0,1:T(8,128)(2,1)} collective-permute-done((bf16[64,12,1024]{2,0,1:T(8,128)(2,1)S(1)}, bf16[64,12,1024]{2,0,1:T(8,128)(2,1)}, u32[]{:S(2)}, u32[]{:S(2)}) %collective-permute-start.1) | collective-permute-done | bytes 1572896 | tf_op jit(solution)/shard_map/ppermute | solution.py:18
  84.5 2.1 pad_maximum_fusion
  86.7 5.4 %copy.6 = bf16[192,12,1024]{2,1,0:T(8,128)(2,1)} copy(bf16[192,12,1024]{2,0,1:T(8,128)(2,1)S(1)} %pad_maximum_fusion) | data formatting | bytes 9437184 | tf_op jit(solution)/shard_map/while | solution.py:115
  92.1 188.3 %while.10 = (s32[]{:T(128)}, f32[2,512,512]{2,1,0:T(8,128)}, s32[2,512]{1,0:T(2,128)S(1)}, bf16[192,12,1024]{2,1,0:T(8,128)(2,1)}, s32[2,512]{1,0:T(2,128)S(1)},...) while((s32[]{:T(128)}, f32[2,512,512]{2,1,0:T(8,128)}, s32[2,512]{1,0:T(2,128)S(1)}, ...), condition=%wide.region_4.6_spmd, body=%wide.region_3.5_spmd.sunk | while | flops 1126968320 | bytes 200317584 | solution.py:115
  92.1 16.7 %gather_fusion.1 = bf16[512,12,1024]{2,1,0:T(8,128)(2,1)} fusion(bf16[192,12,1024]{2,1,0:T(8,128)(2,1)} %get-tuple-element.160, s32[1024]{0:T(1024)S(1)} %pad_clamp_fusion.5), kind=kCustom, calls=%fused_computation.1.clone.clone.1 | custom fusion | bytes 25167872 | tf_op jit(solution)/shard_map/while/body/eval_jaxpr/jit(_take)/gather | solution.py:73
  108.8 14.5 %broadcast_select_fusion.5 = bf16[512,12,1024]{2,1,0:T(8,128)(2,1)} fusion(bf16[512,12,1024]{2,1,0:T(8,128)(2,1)} %gather_fusion.1, pred[512]{0:T(512)(128)(4,1)S(1)} %compare_and_fusion.5), kind=kLoop, calls=%fused_computation.10.clone.1 | loop fusion | flops 6291456 | bytes 25166336 | tf_op jit(solution)/shard_map/while/body/eval_jaxpr/jit(_take)/select_n | solution.py:73
  123.3 16.7 %gather_fusion = bf16[512,12,1024]{2,1,0:T(8,128)(2,1)} fusion(bf16[192,12,1024]{2,1,0:T(8,128)(2,1)} %get-tuple-element.160, s32[1024]{0:T(1024)S(1)} %pad_clamp_fusion.4), kind=kCustom, calls=%fused_computation.clone.clone.1 | custom fusion | bytes 25167872 | tf_op jit(solution)/shard_map/while/body/eval_jaxpr/jit(_take)/gather | solution.py:72
  140.0 15.5 %broadcast_select_fusion.4 = bf16[512,12,1024]{2,1,0:T(8,128)(2,1)} fusion(bf16[512,12,1024]{2,1,0:T(8,128)(2,1)} %gather_fusion, pred[512]{0:T(512)(128)(4,1)S(1)} %compare_and_fusion.4), kind=kLoop, calls=%fused_computation.11.clone.1 | loop fusion | flops 6291456 | bytes 25166336 | tf_op jit(solution)/shard_map/while/body/eval_jaxpr/jit(_take)/select_n | solution.py:72
  155.5 1.3 copy-done
  156.8 25.5 %fusion.55 = (f32[512,512]{1,0:T(8,128)S(1)}, f32[512,512]{1,0:T(8,128)S(1)}, f32[512,512]{1,0:T(8,128)S(1)}, f32[512,512]{1,0:T(8,128)S(1)}) fusion(bf16[512,12,1024]{2,1,0:T(8,128)(2,1)} %broadcast_select_fusion.4, bf16[512,12,1024]{2,1,0:T(8,128)(2,1)S(1)} %copy-done), kind=kLoop, calls=%fused_computation.8.clone.1 | loop fusion | flops 36700160 | bytes 29360128 | tf_op jit(solution)/shard_map/while/body/eval_jaxpr/psk,psk->pk/dot_general | solution.py:79
  182.3 0.2 add.172
  182.6 0.0 copy-start.1
  182.6 0.2 sub.53
  182.8 1.0 copy-done.1
  183.8 0.7 fusion.56
  184.5 1.7 fusion.57
  186.3 16.7 %gather_fusion.1 = bf16[512,12,1024]{2,1,0:T(8,128)(2,1)} fusion(bf16[192,12,1024]{2,1,0:T(8,128)(2,1)} %get-tuple-element.160, s32[1024]{0:T(1024)S(1)} %pad_clamp_fusion.5), kind=kCustom, calls=%fused_computation.1.clone.clone.1 | custom fusion | bytes 25167872 | tf_op jit(solution)/shard_map/while/body/eval_jaxpr/jit(_take)/gather | solution.py:73
  202.9 14.5 %broadcast_select_fusion.5 = bf16[512,12,1024]{2,1,0:T(8,128)(2,1)} fusion(bf16[512,12,1024]{2,1,0:T(8,128)(2,1)} %gather_fusion.1, pred[512]{0:T(512)(128)(4,1)S(1)} %compare_and_fusion.5), kind=kLoop, calls=%fused_computation.10.clone.1 | loop fusion | flops 6291456 | bytes 25166336 | tf_op jit(solution)/shard_map/while/body/eval_jaxpr/jit(_take)/select_n | solution.py:73
  217.4 16.7 %gather_fusion = bf16[512,12,1024]{2,1,0:T(8,128)(2,1)} fusion(bf16[192,12,1024]{2,1,0:T(8,128)(2,1)} %get-tuple-element.160, s32[1024]{0:T(1024)S(1)} %pad_clamp_fusion.4), kind=kCustom, calls=%fused_computation.clone.clone.1 | custom fusion | bytes 25167872 | tf_op jit(solution)/shard_map/while/body/eval_jaxpr/jit(_take)/gather | solution.py:72
  234.1 15.5 %broadcast_select_fusion.4 = bf16[512,12,1024]{2,1,0:T(8,128)(2,1)} fusion(bf16[512,12,1024]{2,1,0:T(8,128)(2,1)} %gather_fusion, pred[512]{0:T(512)(128)(4,1)S(1)} %compare_and_fusion.4), kind=kLoop, calls=%fused_computation.11.clone.1 | loop fusion | flops 6291456 | bytes 25166336 | tf_op jit(solution)/shard_map/while/body/eval_jaxpr/jit(_take)/select_n | solution.py:72
  249.7 1.3 copy-done
  251.0 25.5 %fusion.55 = (f32[512,512]{1,0:T(8,128)S(1)}, f32[512,512]{1,0:T(8,128)S(1)}, f32[512,512]{1,0:T(8,128)S(1)}, f32[512,512]{1,0:T(8,128)S(1)}) fusion(bf16[512,12,1024]{2,1,0:T(8,128)(2,1)} %broadcast_select_fusion.4, bf16[512,12,1024]{2,1,0:T(8,128)(2,1)S(1)} %copy-done), kind=kLoop, calls=%fused_computation.8.clone.1 | loop fusion | flops 36700160 | bytes 29360128 | tf_op jit(solution)/shard_map/while/body/eval_jaxpr/psk,psk->pk/dot_general | solution.py:79
  276.5 0.2 add.172
  276.7 0.0 copy-start.1
  276.7 0.2 sub.53
  276.9 1.0 copy-done.1
  277.9 0.7 fusion.56
  278.7 1.7 fusion.57
  280.4 3.1 %bitcast_select_fusion = f32[1024,512]{1,0:T(8,128)} fusion(f32[2,512,512]{2,1,0:T(8,128)} %get-tuple-element.43, pred[1024]{0:T(1024)(128)(4,1)S(1)} %copy-done.3), kind=kLoop, calls=%fused_computation.40 | loop fusion | flops 524288 | bytes 4195328 | tf_op jit(solution)/shard_map/jit(_where)/select_n | solution.py:121
  (30 shorter events, 0.3 us)
Async XLA Ops:
  2.1 21.4 %all-to-all-start = ((bf16[3,16,64,128]{3,2,0,1:T(8,128)(2,1)}), bf16[3,16,64,128]{3,2,0,1:T(8,128)(2,1)S(1)}, u32[]{:S(2)}, u32[]{:S(2)}) async-start(bf16[3,16,64,128]{3,2,0,1:T(8,128)(2,1)} %copy.5), calls=%async_computation | async-start | bytes 1572864 | tf_op jit(solution)/shard_map/all_to_all | solution.py:94
  26.8 4.6 %copy-start.2 = (s32[2,1024]{1,0:T(2,128)S(1)}, s32[2,1024]{1,0:T(2,128)}, u32[]{:S(2)}) copy-start(s32[2,1024]{1,0:T(2,128)} %param.8) | copy-start | bytes 24580
  27.3 34.9 %collective-permute-start = (bf16[64,12,1024]{2,0,1:T(8,128)(2,1)S(1)}, bf16[64,12,1024]{2,0,1:T(8,128)(2,1)}, u32[]{:S(2)}, u32[]{:S(2)}) collective-permute-start(bf16[64,12,1024]{2,0,1:T(8,128)(2,1)S(1)} %multiply_convert_fusion), channel_id=1, source_target_pairs={{1,0},{2,1},{3,2},{4,3},{5,4},{6,5},{7,6},{8,7},{9,8},{10,9},{11,1... | collective-permute-start | bytes 4718600 | tf_op jit(solution)/shard_map/ppermute | solution.py:18
  29.2 55.3 %collective-permute-start.1 = (bf16[64,12,1024]{2,0,1:T(8,128)(2,1)S(1)}, bf16[64,12,1024]{2,0,1:T(8,128)(2,1)}, u32[]{:S(2)}, u32[]{:S(2)}) collective-permute-start(bf16[64,12,1024]{2,0,1:T(8,128)(2,1)S(1)} %multiply_convert_fusion), channel_id=1, source_target_pairs={{2,0},{3,1},{4,2},{5,3},{6,4},{7,5},{8,6},{9,7},{10,8},{11,9},{12,... | collective-permute-start | bytes 4718600 | tf_op jit(solution)/shard_map/ppermute | solution.py:18
  92.1 188.3 %copy-start.3 = (pred[1024]{0:T(1024)(128)(4,1)S(1)}, pred[1024]{0:T(1024)(128)(4,1)}, u32[]{:S(2)}) copy-start(pred[1024]{0:T(1024)(128)(4,1)} %iota_compare_fusion) | copy-start | bytes 3076
  140.0 16.9 %copy-start = (bf16[512,12,1024]{2,1,0:T(8,128)(2,1)S(1)}, bf16[512,12,1024]{2,1,0:T(8,128)(2,1)}, u32[]{:S(2)}) copy-start(bf16[512,12,1024]{2,1,0:T(8,128)(2,1)} %broadcast_select_fusion.5) | copy-start | bytes 37748740 | tf_op jit(solution)/shard_map/while
  182.6 1.2 copy-start.1
  234.1 16.9 %copy-start = (bf16[512,12,1024]{2,1,0:T(8,128)(2,1)S(1)}, bf16[512,12,1024]{2,1,0:T(8,128)(2,1)}, u32[]{:S(2)}) copy-start(bf16[512,12,1024]{2,1,0:T(8,128)(2,1)} %broadcast_select_fusion.5) | copy-start | bytes 37748740 | tf_op jit(solution)/shard_map/while
  276.7 1.2 copy-start.1
where the time goes:
time: 284 us; the launch traced here: 283 us
  other arithmetic  129 us (45%)
  local copies, waits for them, and re-layouts  78.9 us (28%)
  waiting for transfers between devices  56.3 us (20%)
  starting transfers between devices  11.2 us (4%)
  matrix products  6.98 us (2%)
    dot_general x2, other arithmetic, correlate(): jnp.einsum('psk,psk->pk', left_imag, right_imag, preferred_element_type=j...  51 us
    ppermute x2, waiting for transfers between devices, from_behind(): return lax.ppermute(block, axis, route)  46.1 us
    gather x2, local copies, waits for them, and re-layouts, correlate(): right_rows = jnp.take(spectra, seconds, axis=0)  33.4 us
    gather x2, local copies, waits for them, and re-layouts, correlate(): left_rows = jnp.take(spectra, firsts, axis=0)  33.4 us
    select_n x4, other arithmetic, correlate(): left_rows = jnp.take(spectra, firsts, axis=0)  31.1 us
    select_n x4, other arithmetic, correlate(): right_rows = jnp.take(spectra, seconds, axis=0)  28.9 us
    all_to_all x1, waiting for transfers between devices, per_device(): lax.all_to_all(panels, 'tm', split_axis=1, concat_axis=0, tiled=True)  10.1 us
    all_to_all x1, starting transfers between devices, per_device(): lax.all_to_all(panels, 'tm', split_axis=1, concat_axis=0, tiled=True)  7.03 us
  transfers between devices with their start and end apart: 3, of which 3 were waited for; matrix products, arithmetic and copies ran while one was open for 4% of the time, Pallas kernels for 0%

commit v1 on v0

v1 whole, which is shorter than its diff:
```python
import math
import numpy as np
import ml_dtypes
import jax, jax.numpy as jnp
from jax import lax
from jax.sharding import PartitionSpec as P
from jax.experimental import pallas as pl
from jax.experimental.pallas import tpu as pltpu

SEG=512; SEGS=12; CAP=1024
def tables():
    u=np.arange(SEG)[:,None]; k=np.arange(SEG)[None,:]
    a=(u*k%(2*SEG))*(math.pi/SEG)
    fwd=np.concatenate([np.cos(a),-np.sin(a)],axis=1)/math.sqrt(SEG)
    k=np.arange(SEG)[:,None]; m=np.arange(SEG)[None,:]-SEG//2
    a=(k*m%(2*SEG))*(math.pi/SEG)
    w=np.where(k==0,1.0,2.0)/math.sqrt(SEG)/SEGS
    inv=np.concatenate([w*np.cos(a),-w*np.sin(a)],axis=0)
    return fwd.astype(np.float32).astype(ml_dtypes.bfloat16), inv.astype(np.float32).astype(ml_dtypes.bfloat16)

NCH=168
MB=336
U=8
ROWS=SEGS*8
def kernel(idx_ref, cnt_ref, own_ref, h1_ref, h2_ref, fwd_ref, inv_ref, out_ref, scaled, spec, cr, ci):
    for s in range(SEGS):
        base=0
        for ref in (own_ref,h1_ref,h2_ref):
            C=ref.shape[1]
            x=[ref[4*s+q].astype(jnp.float32) for q in range(4)]
            ss=x[0]*x[0]+x[1]*x[1]+x[2]*x[2]+x[3]*x[3]
            g=lax.rsqrt(jnp.sum(ss,axis=1,keepdims=True)*(1.0/SEG)+1e-5)
            for q in range(4):
                scaled[pl.ds(s*NCH+base,C),q*128:(q+1)*128]=(x[q]*g).astype(jnp.bfloat16)
            base+=C
    for b in range(SEGS*NCH//MB):
        spectrum=jnp.dot(scaled[pl.ds(b*MB,MB),:],fwd_ref[...],preferred_element_type=jnp.float32)
        for t in range(MB//NCH):
            s=b*(MB//NCH)+t
            for c in range(8):
                part,g=divmod(c,4)
                row=(part*6+s//2)*8+(s%2)*4+g
                spec[pl.ds(row,NCH,stride=ROWS),:]=spectrum[t*NCH:(t+1)*NCH,c*128:(c+1)*128]
    def whiten(ch,_):
        v=[spec[pl.ds(ch*ROWS+r*8,8),:] for r in range(12)]
        lev=v[0]*v[0]
        for r in range(1,12): lev=lev+v[r]*v[r]
        lev=lev+pltpu.roll(lev,4,0)
        g=lax.rsqrt(lev*(1.0/SEGS)+0.5)
        for r in range(12):
            spec[pl.ds(ch*ROWS+r*8,8),:]=v[r]*g
        return 0
    lax.fori_loop(0,NCH,whiten,0,unroll=4)
    def pairs(n,_):
        for t in range(U):
            p=n*U+t
            i=pl.multiple_of(idx_ref[0,p],8); j=pl.multiple_of(idx_ref[1,p],8)
            are=None
            for h in range(6):
                lr=spec[pl.ds(i+h*8,8),:]; li=spec[pl.ds(i+(6+h)*8,8),:]
                rr=spec[pl.ds(j+h*8,8),:]; ri=spec[pl.ds(j+(6+h)*8,8),:]
                if are is None:
                    are=lr*rr+li*ri; aim=li*rr-lr*ri
                else:
                    are=are+lr*rr+li*ri; aim=aim+li*rr-lr*ri
            cr[pl.ds(p*8,8),:]=are
            ci[pl.ds(p*8,8),:]=aim
        return 0
    lax.fori_loop(0,CAP//U,pairs,0)
    PB=256
    for b in range(CAP//PB):
        cols=[]
        for ref in (cr,ci):
            for g in range(4):
                a=ref[pl.ds(b*PB*8+g,PB,stride=8),:]+ref[pl.ds(b*PB*8+g+4,PB,stride=8),:]
                cols.append(a.astype(jnp.bfloat16))
        x=jnp.concatenate(cols,axis=1)
        y=jnp.dot(x,inv_ref[...],preferred_element_type=jnp.float32)
        slot=lax.broadcasted_iota(jnp.int32,(PB,SEG),0)+b*PB
        out_ref[pl.ds(b*PB,PB),:]=jnp.where(slot<cnt_ref[0],y,0.0)

def correlate(idx, cnt, own, h1, h2, fwd, inv):
    V=pl.BlockSpec(memory_space=pltpu.VMEM); S=pl.BlockSpec(memory_space=pltpu.SMEM)
    return pl.pallas_call(kernel,out_shape=jax.ShapeDtypeStruct((CAP,SEG),jnp.float32),
      in_specs=[S,S,V,V,V,V,V],out_specs=V,
      scratch_shapes=[pltpu.VMEM((SEGS*NCH,SEG),jnp.bfloat16),pltpu.VMEM((NCH*ROWS,128),jnp.float32),
         pltpu.VMEM((CAP*8,128),jnp.float32),pltpu.VMEM((CAP*8,128),jnp.float32)],
      compiler_params=pltpu.CompilerParams(vmem_limit_bytes=48<<20))(idx,cnt,own,h1,h2,fwd,inv)


def from_ahead(block, axis, distance):
    devices = range(lax.axis_size(axis))
    route = [(i + distance, i) for i in devices if i + distance in devices]
    return lax.ppermute(block, axis, route)


def per_device(panels, pair_list, pair_count):
    relaid = lax.all_to_all(panels, "tm", split_axis=1, concat_axis=0, tiled=True)
    own = relaid[:, 0]
    channels = own.shape[1]
    h1 = from_ahead(own, "pairs", 1)
    h2 = from_ahead(own[:, :NCH - 2 * channels], "pairs", 2)
    fwd, inv = tables()
    offset = (lax.axis_index("tm") * lax.axis_size("pairs") + lax.axis_index("pairs")) * channels
    idx = (pair_list - offset) * ROWS
    return correlate(idx, pair_count, own, h1, h2, jnp.asarray(fwd), jnp.asarray(inv))


def solution(mesh):
    return jax.shard_map(
        per_device,
        mesh=mesh,
        in_specs=(P("tm", None, "pairs", None), P(None, ("tm", "pairs")), P(("tm", "pairs"))),
        out_specs=P(("tm", "pairs"), None),
        check_vma=False,
    )
```

time: 284 us -> 68.3 us (0.24)
  other arithmetic: 129 us -> 0.01 us
  local copies, waits for them, and re-layouts: 78.9 us -> 2.18 us
  waiting for transfers between devices: 56.3 us -> 20.1 us
  blocking collectives: 0 us -> 21 us
  Pallas kernels: 0 us -> 20.2 us
  starting transfers between devices: 11.2 us -> 3.91 us
  matrix products: 6.98 us -> 0 us
    gather x4 -> x0, local copies, waits for them, and re-layouts: 66.7 us -> none  [the longest x2 33.4 us: correlate(): right_rows = jnp.take(spectra, seconds, axis=0)]
    select_n x9 -> x0, other arithmetic: 63.2 us -> none  [the longest x4 31.1 us: correlate(): left_rows = jnp.take(spectra, firsts, axis=0)]
    dot_general x2 -> x0, other arithmetic: 51 us -> none  [correlate(): jnp.einsum('psk,psk->pk', left_imag, right_imag, preferred_element_type=j...]
    ppermute x2, waiting for transfers between devices: 46.1 us -> 20.1 us  [from_ahead(): return lax.ppermute(block, axis, route)]
    all_to_all x0 -> x1, blocking collectives: none -> 21 us  [per_device(): lax.all_to_all(panels, 'tm', split_axis=1, concat_axis=0, tiled=True)]
    pallas_call x0 -> x1, Pallas kernels: none -> 20.2 us  [correlate(): pl.pallas_call(kernel, out_shape=jax.ShapeDtypeStruct((CAP, SEG), jnp.flo...]
    all_to_all x1 -> x0, waiting for transfers between devices: 10.1 us -> none  [per_device(): lax.all_to_all(panels, 'tm', split_axis=1, concat_axis=0, tiled=True)]
    while x9 -> x0, local copies, waits for them, and re-layouts: 10.1 us -> none  [the longest x1 5.42 us: per_device(): lax.map(one_block, (firsts.reshape(block_total, PAIR_BLOCK), seconds.resh...]
  transfers between devices with their start and end apart: 3 -> 2, of which waited for: 3 -> 1; matrix products, arithmetic and copies ran while one was open for 4% -> 1% of each run, Pallas kernels for 0% -> 0%
where the time goes in v1:
time: 68.3 us; the launch traced here: 68.1 us
  blocking collectives  21 us (31%)
  Pallas kernels  20.2 us (30%)
  waiting for transfers between devices  20.1 us (29%)
  starting transfers between devices  3.91 us (6%)
  local copies, waits for them, and re-layouts  2.18 us (3%)
  between operations  0.7 us (1%)
    all_to_all x1, blocking collectives, per_device(): lax.all_to_all(panels, 'tm', split_axis=1, concat_axis=0, tiled=True)  21 us
    pallas_call x1, Pallas kernels, correlate(): pl.pallas_call(kernel, out_shape=jax.ShapeDtypeStruct((CAP, SEG), jnp.flo...  20.2 us
    ppermute x2, waiting for transfers between devices, from_ahead(): return lax.ppermute(block, axis, route)  20.1 us
    ppermute x2, starting transfers between devices, from_ahead(): return lax.ppermute(block, axis, route)  3.91 us
  transfers between devices with their start and end apart: 2, of which 1 were waited for; matrix products, arithmetic and copies ran while one was open for 1% of the time, Pallas kernels for 0%

profile of v1, /device:TPU:96, one launch (start us, length us, event | category | flops | bytes accessed | tf_op | source)
XLA Modules:
  0.0 68.1 jit_solution(13955716261752110509)
XLA Ops:
  0.0 0.0 copy-start
  0.0 0.0 copy-start.1
  0.0 0.0 copy-start.2
  0.0 1.3 %copy.7 = bf16[3,16,64,128]{3,2,0,1:T(8,128)(2,1)S(1)} copy(bf16[3,16,64,128]{3,2,1,0:T(8,128)(2,1)} %param.5) | data formatting | bytes 1572864 | tf_op args[0]
  1.4 21.0 %all_to_all.15 = bf16[3,16,64,128]{3,2,0,1:T(8,128)(2,1)S(1)} all-to-all(bf16[3,16,64,128]{3,2,0,1:T(8,128)(2,1)S(1)} %copy.7), channel_id=1, replica_groups=mesh['tm'=16,'pairs'=16] {'tm'}, dimensions={1} | all-to-all | bytes 1572864 | tf_op jit(solution)/shard_map/all_to_all | solution.py:98
  22.3 1.9 %collective-permute-start = (bf16[48,64,128]{2,1,0:T(8,128)(2,1)S(1)}, bf16[48,64,128]{2,1,0:T(8,128)(2,1)}, u32[]{:S(2)}, u32[]{:S(2)}) collective-permute-start(bf16[48,64,128]{2,1,0:T(8,128)(2,1)S(1)} %bitcast.5), channel_id=1, source_target_pairs={{1,0},{2,1},{3,2},{4,3},{5,4},{6,5},{7,6},{8,7},{9,8},{10,9},{11,1... | collective-permute-start | bytes 2359304 | tf_op jit(solution)/shard_map/ppermute | solution.py:94
  24.2 0.8 %slice.4 = bf16[48,40,128]{2,1,0:T(8,128)(2,1)} slice(bf16[48,64,128]{2,1,0:T(8,128)(2,1)S(1)} %bitcast.6), slice={[0:48], [0:40], [0:128]} | slice | bytes 983040 | tf_op jit(solution)/shard_map/slice | solution.py:102
  25.1 2.0 %collective-permute-start.1 = (bf16[48,40,128]{2,1,0:T(8,128)(2,1)}, bf16[48,40,128]{2,1,0:T(8,128)(2,1)S(1)}, u32[]{:S(2)}, u32[]{:S(2)}) collective-permute-start(bf16[48,40,128]{2,1,0:T(8,128)(2,1)} %slice.4), channel_id=1, source_target_pairs={{2,0},{3,1},{4,2},{5,3},{6,4},{7,5},{8,6},{9,7},{10,8},{11,9},{12,... | collective-permute-start | bytes 1474568 | tf_op jit(solution)/shard_map/ppermute | solution.py:94
  27.7 0.0 copy-done.2
  27.8 20.1 %collective-permute-done.1.h2_ref = bf16[48,40,128]{2,1,0:T(8,128)(2,1)S(1)} collective-permute-done((bf16[48,40,128]{2,1,0:T(8,128)(2,1)}, bf16[48,40,128]{2,1,0:T(8,128)(2,1)S(1)}, u32[]{:S(2)}, u32[]{:S(2)}) %collective-permute-start.1) | collective-permute-done | bytes 491552 | tf_op jit(solution)/shard_map/ppermute | solution.py:94
  47.8 0.0 collective-permute-done.h1_ref
  47.8 0.0 copy-done
  47.8 0.0 copy-done.1
  47.8 20.2 %shard_map.55 = f32[1024,512]{1,0:T(8,128)} custom-call(s32[2,1024]{1,0:T(2,128)S(1)} %subtract_multiply_fusion.idx_ref, s32[1]{0:T(128)S(6)} %copy.8.cnt_ref, bf16[48,64,128]{2,1,0:T(8,128)(2,1)S(1)} %bitcast.7, bf16[48,64,128]{2,1,0:T(8,128)(2,1)} %collective-permute-done.h1_ref, bf16[48,40,128]{2,1,0:T(8,128)(2,1)S(1)} %collective-permute-done.1.h2_ref, ...), custom_call_target="tpu_custom_call" | custom-call | tf_op jit(solution)/shard_map/pallas_call | solution.py:84
  (1 shorter events, 0.0 us)
Async XLA Ops:
  0.0 47.8 %copy-start = (bf16[1024,512]{1,0:T(8,128)(2,1)S(1)}, bf16[1024,512]{1,0:T(8,128)(2,1)}, u32[]{:S(2)}) copy-start(bf16[1024,512]{1,0:T(8,128)(2,1)} %constant.18.clone.inv_ref) | copy-start | bytes 3145732
  0.0 47.8 %copy-start.1 = (bf16[512,1024]{1,0:T(8,128)(2,1)S(1)}, bf16[512,1024]{1,0:T(8,128)(2,1)}, u32[]{:S(2)}) copy-start(bf16[512,1024]{1,0:T(8,128)(2,1)} %constant.17.clone.fwd_ref) | copy-start | bytes 3145732
  0.0 27.7 %copy-start.2 = (s32[2,1024]{1,0:T(2,128)S(1)}, s32[2,1024]{1,0:T(2,128)}, u32[]{:S(2)}) copy-start(s32[2,1024]{1,0:T(2,128)} %param.6) | copy-start | bytes 24580
  22.3 25.5 %collective-permute-start = (bf16[48,64,128]{2,1,0:T(8,128)(2,1)S(1)}, bf16[48,64,128]{2,1,0:T(8,128)(2,1)}, u32[]{:S(2)}, u32[]{:S(2)}) collective-permute-start(bf16[48,64,128]{2,1,0:T(8,128)(2,1)S(1)} %bitcast.5), channel_id=1, source_target_pairs={{1,0},{2,1},{3,2},{4,3},{5,4},{6,5},{7,6},{8,7},{9,8},{10,9},{11,1... | collective-permute-start | bytes 2359304 | tf_op jit(solution)/shard_map/ppermute | solution.py:94
  25.1 22.8 %collective-permute-start.1 = (bf16[48,40,128]{2,1,0:T(8,128)(2,1)}, bf16[48,40,128]{2,1,0:T(8,128)(2,1)S(1)}, u32[]{:S(2)}, u32[]{:S(2)}) collective-permute-start(bf16[48,40,128]{2,1,0:T(8,128)(2,1)} %slice.4), channel_id=1, source_target_pairs={{2,0},{3,1},{4,2},{5,3},{6,4},{7,5},{8,6},{9,7},{10,8},{11,9},{12,... | collective-permute-start | bytes 1474568 | tf_op jit(solution)/shard_map/ppermute | solution.py:94

commit v2 on v1

v2 whole, which is shorter than its diff:
```python
import math

import jax
import jax.numpy as jnp
import ml_dtypes
import numpy as np
from jax import lax
from jax.experimental import pallas as pl
from jax.experimental.pallas import tpu as pltpu
from jax.sharding import PartitionSpec as P

NB = 100
SEG = 512
SEGS = 12
TILE = 128
QUADS = SEG // TILE
OWN = 64
HALO = 104
REST = HALO - OWN
ROWS = SEGS * 8
PITCH = ROWS + 1
CAP = 1024
UNROLL = 16
JOBS = CAP + UNROLL
BLOCK = 256
VMEM = pl.BlockSpec(memory_space=pltpu.VMEM)
SMEM = pl.BlockSpec(memory_space=pltpu.SMEM)
HBM = pl.BlockSpec(memory_space=pltpu.HBM)


def tables():
    left = np.arange(SEG)[:, None]
    right = np.arange(SEG)[None, :]
    angles = (left * right % (2 * SEG)) * (math.pi / SEG)
    forward = np.concatenate([np.cos(angles), -np.sin(angles)], axis=1) / math.sqrt(SEG)
    angles = (left * (right - SEG // 2) % (2 * SEG)) * (math.pi / SEG)
    weights = np.where(left == 0, 1.0, 2.0) / (math.sqrt(SEG) * SEGS)
    inverse = np.concatenate([weights * np.cos(angles), -weights * np.sin(angles)], axis=0)
    return forward.astype(ml_dtypes.bfloat16), inverse.astype(ml_dtypes.bfloat16)


def spectra(parts, fwd_ref, scaled, loose, spec):
    total = sum(part.shape[1] for part in parts)
    for s in range(SEGS):
        base = s * total
        for part in parts:
            count = part.shape[1]
            tiles = [part[QUADS * s + q].astype(jnp.float32) for q in range(QUADS)]
            squares = sum(tile * tile for tile in tiles)
            power = jnp.sum(squares, axis=1, keepdims=True) * (1.0 / SEG)
            gain = lax.rsqrt(power + 1e-05)
            for q, tile in enumerate(tiles):
                scaled[pl.ds(base, count), q * TILE:(q + 1) * TILE] = (tile * gain).astype(jnp.bfloat16)
            base += count
    for s in range(0, SEGS, 2):
        rows = scaled[pl.ds(s * total, 2 * total), :]
        both = jnp.dot(rows, fwd_ref[...], preferred_element_type=jnp.float32)
        for t in range(2):
            for c in range(2 * QUADS):
                half, g = divmod(c, QUADS)
                row = (half * (SEGS // 2) + s // 2) * 8 + t * QUADS + g
                loose[pl.ds(row, total, stride=PITCH), :] = both[
                    t * total:(t + 1) * total, c * TILE:(c + 1) * TILE]

    def whiten(ch, carry):
        v = [loose[pl.ds(ch * PITCH + r * 8, 8), :] for r in range(SEGS)]
        level = sum(x * x for x in v)
        level = level + pltpu.roll(level, 4, 0)
        gain = lax.rsqrt(level * (1.0 / SEGS) + 0.5)
        for r in range(SEGS):
            spec[pl.ds(pl.multiple_of(ch * ROWS + r * 8, 8), 8), :] = v[r] * gain
        return carry

    lax.fori_loop(0, total, whiten, 0, unroll=4)


def pair_products(job_ref, left_spec, right_spec, cross):
    low_half = lax.broadcasted_iota(jnp.int32, (8, TILE), 0) < QUADS

    def step(n, carry):
        for t in range(UNROLL):
            slot = n * UNROLL + t
            i = pl.multiple_of(job_ref[slot], 8)
            j = pl.multiple_of(job_ref[JOBS + slot], 8)
            row = pl.multiple_of(job_ref[2 * JOBS + slot], 8)
            real = imag = None
            for h in range(SEGS // 2):
                lr = left_spec[pl.ds(i + h * 8, 8), :]
                li = left_spec[pl.ds(i + (SEGS // 2 + h) * 8, 8), :]
                rr = right_spec[pl.ds(j + h * 8, 8), :]
                ri = right_spec[pl.ds(j + (SEGS // 2 + h) * 8, 8), :]
                if real is None:
                    real = lr * rr + li * ri
                    imag = li * rr - lr * ri
                else:
                    real = real + lr * rr + li * ri
                    imag = imag + li * rr - lr * ri
            real = real + pltpu.roll(real, QUADS, 0)
            imag = imag + pltpu.roll(imag, QUADS, 0)
            cross[pl.ds(row, 8), :] = jnp.where(low_half, real, imag)
        return carry

    lax.fori_loop(0, (job_ref[3 * JOBS] + UNROLL - 1) // UNROLL, step, 0)


def order_kernel(pairs_ref, live_ref, offset_ref, near_ref, far_ref):
    offset = offset_ref[0]
    live = live_ref[0]

    def step(p, carry):
        near, far = carry
        i = (pairs_ref[0, p] - offset) * ROWS
        j = (pairs_ref[1, p] - offset) * ROWS
        inside = (j < OWN * ROWS).astype(jnp.int32)
        active = (p < live).astype(jnp.int32)
        near_ref[near] = i
        near_ref[JOBS + near] = jnp.minimum(j, (OWN - 1) * ROWS)
        near_ref[2 * JOBS + near] = p * 8
        far_ref[far] = i
        far_ref[JOBS + far] = jnp.maximum(j - OWN * ROWS, 0)
        far_ref[2 * JOBS + far] = p * 8
        near = near + active * inside
        return near, far + active - active * inside

    near, far = lax.fori_loop(0, CAP, step, (jnp.int32(0), jnp.int32(0)), unroll=8)
    for ref, count in ((near_ref, near), (far_ref, far)):
        for t in range(UNROLL):
            ref[count + t] = 0
            ref[JOBS + count + t] = 0
            ref[2 * JOBS + count + t] = CAP * 8
        ref[3 * JOBS] = count
        ref[3 * JOBS + 1] = live


def near_kernel(job_ref, own_ref, fwd_ref, spec_out, cross_out, scaled, loose, spec, cross, sems):
    spectra([own_ref], fwd_ref, scaled, loose, spec)
    spec_copy = pltpu.make_async_copy(spec, spec_out, sems.at[0])
    spec_copy.start()
    pair_products(job_ref, spec, spec, cross)
    cross_copy = pltpu.make_async_copy(cross, cross_out, sems.at[1])
    cross_copy.start()
    spec_copy.wait()
    cross_copy.wait()


def far_kernel(job_ref, h1_ref, h2_ref, spec_in, cross_in, fwd_ref, inv_ref, out_ref,
               scaled, loose, halo, spec, cross, stacks, sems):
    spec_copy = pltpu.make_async_copy(spec_in, spec, sems.at[0])
    cross_copy = pltpu.make_async_copy(cross_in, cross, sems.at[1])
    spec_copy.start()
    cross_copy.start()
    spectra([h1_ref, h2_ref], fwd_ref, scaled, loose, halo)
    spec_copy.wait()
    cross_copy.wait()
    pair_products(job_ref, spec, halo, cross)
    live = job_ref[3 * JOBS + 1]
    copies = []
    for b in range(CAP // BLOCK):
        rows = pl.ds(b * BLOCK, BLOCK)

        @pl.when(b * BLOCK < live)
        def _():
            columns = [cross[pl.ds(b * BLOCK * 8 + g, BLOCK, stride=8), :].astype(jnp.bfloat16) for g in range(8)]
            lagged = jnp.dot(
                jnp.concatenate(columns, axis=1), inv_ref[...], preferred_element_type=jnp.float32)
            slot = lax.broadcasted_iota(jnp.int32, (BLOCK, SEG), 0) + b * BLOCK
            stacks[rows, :] = jnp.where(slot < live, lagged, 0.0)

        @pl.when(b * BLOCK >= live)
        def _():
            stacks[rows, :] = jnp.zeros((BLOCK, SEG), jnp.float32)

        copies.append(pltpu.make_async_copy(stacks.at[rows, :], out_ref.at[rows, :], sems.at[2 + b]))
        copies[-1].start()
    for copy in copies:
        copy.wait()


def ints(*shape):
    return jax.ShapeDtypeStruct(shape, jnp.int32)


def floats(*shape):
    return jax.ShapeDtypeStruct(shape, jnp.float32)


CROSS = ((CAP + 1) * 8, TILE)


def order_pairs(pair_list, live, offset):
    return pl.pallas_call(
        order_kernel,
        out_shape=(ints(3 * JOBS + 16), ints(3 * JOBS + 16)),
        in_specs=[SMEM] * 3,
        out_specs=(SMEM,) * 2,
        name="order_pairs",
    )(pair_list, live, offset)


def near_pairs(jobs, own, fwd):
    return pl.pallas_call(
        near_kernel,
        out_shape=(floats(OWN * ROWS, TILE), floats(*CROSS)),
        in_specs=[SMEM, VMEM, VMEM],
        out_specs=(HBM,) * 2,
        scratch_shapes=[
            pltpu.VMEM((SEGS * OWN, SEG), jnp.bfloat16),
            pltpu.VMEM((OWN * PITCH + 8, TILE), jnp.float32),
            pltpu.VMEM((OWN * ROWS, TILE), jnp.float32),
            pltpu.VMEM(CROSS, jnp.float32),
            pltpu.SemaphoreType.DMA((2,)),
        ],
        compiler_params=pltpu.CompilerParams(vmem_limit_bytes=60 << 20),
        name="near_pairs",
    )(jobs, own, fwd)


def far_pairs(jobs, h1, h2, spec, cross, fwd, inv):
    return pl.pallas_call(
        far_kernel,
        out_shape=floats(CAP, SEG),
        in_specs=[SMEM, VMEM, VMEM, HBM, HBM, VMEM, VMEM],
        out_specs=HBM,
        scratch_shapes=[
            pltpu.VMEM((SEGS * HALO, SEG), jnp.bfloat16),
            pltpu.VMEM((HALO * PITCH + 8, TILE), jnp.float32),
            pltpu.VMEM((HALO * ROWS, TILE), jnp.float32),
            pltpu.VMEM((OWN * ROWS, TILE), jnp.float32),
            pltpu.VMEM(CROSS, jnp.float32),
            pltpu.VMEM((CAP, SEG), jnp.float32),
            pltpu.SemaphoreType.DMA((2 + CAP // BLOCK,)),
        ],
        compiler_params=pltpu.CompilerParams(vmem_limit_bytes=60 << 20),
        name="far_pairs",
    )(jobs, h1, h2, spec, cross, fwd, inv)


def from_ahead(block, axis, distance):
    devices = range(lax.axis_size(axis))
    route = [(i + distance, i) for i in devices if i + distance in devices]
    return lax.ppermute(block, axis, route)


def by_section(block):
    rows = lax.all_to_all(block, "tm", split_axis=0, concat_axis=0, tiled=True)
    return rows.reshape(-1, *block.shape[2:])


def per_device(panels, pair_list, pair_count):
    fwd, inv = (jnp.asarray(table) for table in tables())
    offset = (lax.axis_index("tm") * lax.axis_size("pairs") + lax.axis_index("pairs")) * OWN
    near, far = order_pairs(pair_list, pair_count, offset.astype(jnp.int32)[None])
    turned = jnp.transpose(panels, (1, 0, 2, 3))
    h2_turned = from_ahead(turned[:, :, :REST], "pairs", 2)
    own = by_section(turned)
    own, near, far = lax.optimization_barrier((own, near, far))
    h1 = from_ahead(own, "pairs", 1)
    h2 = by_section(h2_turned)
    spec, cross = near_pairs(near, own, fwd)
    return far_pairs(far, h1, h2, spec, cross, fwd, inv)


def solution(mesh):
    return jax.shard_map(
        per_device,
        mesh=mesh,
        in_specs=(P("tm", None, "pairs", None), P(None, ("tm", "pairs")), P(("tm", "pairs"))),
        out_specs=P(("tm", "pairs"), None),
        check_vma=False,
    )
```

time: 68.3 us -> 61.8 us (0.905)
  the two profiles are of different devices: /device:TPU:96 before, /device:TPU:224 now
where the time goes in v2:
time: 61.8 us; the launch traced here: 61.5 us
  Pallas kernels  31.8 us (51%)
  starting transfers between devices  19.9 us (32%)
  waiting for transfers between devices  4.77 us (8%)
  local copies, waits for them, and re-layouts  4.29 us (7%)
  between operations  0.73 us (1%)
    all_to_all x2, starting transfers between devices, by_section(): rows = lax.all_to_all(block, 'tm', split_axis=0, concat_axis=0, tiled=True)  14.3 us
    pallas_call x1, Pallas kernels, order_pairs(): pl.pallas_call(order_kernel, out_shape=(ints(3 * JOBS + 16), ints(3 * JOB...  13.5 us
    pallas_call x1, Pallas kernels, far_pairs(): pl.pallas_call(far_kernel, out_shape=floats(CAP, SEG), in_specs=[SMEM, VM...  11.2 us
    pallas_call x1, Pallas kernels, near_pairs(): pl.pallas_call(near_kernel, out_shape=(floats(OWN * ROWS, TILE), floats(*...  7.07 us
    ppermute x2, starting transfers between devices, from_ahead(): return lax.ppermute(block, axis, route)  5.62 us
    all_to_all x2, waiting for transfers between devices, by_section(): rows = lax.all_to_all(block, 'tm', split_axis=0, concat_axis=0, tiled=True)  4.76 us
    unnamed x7, local copies, waits for them, and re-layouts  3.17 us
  transfers between devices with their start and end apart: 4, of which 1 were waited for; matrix products, arithmetic and copies ran while one was open for 2% of the time, Pallas kernels for 33%

profile of v2, /device:TPU:224, one launch (start us, length us, event | category | flops | bytes accessed | tf_op | source)
XLA Modules:
  0.0 61.5 jit_solution(6711190128955847854)
XLA Ops:
  0.0 2.1 %copy.10 = bf16[3,16,64,128]{3,2,0,1:T(8,128)(2,1)} copy(bf16[3,16,64,128]{3,2,1,0:T(8,128)(2,1)} %param.5) | data formatting | bytes 1572864 | tf_op args[0]
  2.1 7.0 %all-to-all-start = ((bf16[16,3,64,128]{3,2,1,0:T(8,128)(2,1)}), bf16[16,3,64,128]{3,2,1,0:T(8,128)(2,1)S(1)}, u32[]{:S(2)}, u32[]{:S(2)}) async-start(bf16[16,3,64,128]{3,2,1,0:T(8,128)(2,1)} %bitcast.5), calls=%async_computation | async-start | bytes 1572864 | tf_op jit(solution)/shard_map/all_to_all | solution.py:245
  9.1 1.1 %slice.4 = bf16[16,3,40,128]{3,2,1,0:T(8,128)(2,1)S(1)} slice(bf16[16,3,64,128]{3,2,1,0:T(8,128)(2,1)} %bitcast.5), slice={[0:16], [0:3], [0:40], [0:128]} | slice | bytes 983040 | tf_op jit(solution)/shard_map/slice | solution.py:254
  10.2 3.7 %collective-permute-start.1 = (bf16[16,3,40,128]{3,2,1,0:T(8,128)(2,1)S(1)}, bf16[16,3,40,128]{3,2,1,0:T(8,128)(2,1)}, u32[]{:S(2)}, u32[]{:S(2)}) collective-permute-start(bf16[16,3,40,128]{3,2,1,0:T(8,128)(2,1)S(1)} %slice.4), channel_id=1, source_target_pairs={{2,0},{3,1},{4,2},{5,3},{6,4},{7,5},{8,6},{9,7},{10,8},{11,9},{12,... | collective-permute-start | bytes 1474568 | tf_op jit(solution)/shard_map/ppermute | solution.py:241
  14.6 13.5 %order_pairs.1 = (s32[3136]{0:T(1024)}, s32[3136]{0:T(1024)}) custom-call(s32[2,1024]{1,0:T(2,128)} %pairs_ref.1, s32[1]{0:T(128)S(6)} %copy.11.live_ref, s32[1]{0:T(128)} %bitcast.2.offset_ref), custom_call_target="tpu_custom_call" | custom-call | tf_op jit(solution)/shard_map/order_pairs/pallas_call | solution.py:191
  28.1 0.0 all-to-all-done
  28.1 0.0 copy-start
  28.1 1.9 %collective-permute-start = (bf16[48,64,128]{2,1,0:T(8,128)(2,1)S(1)}, bf16[48,64,128]{2,1,0:T(8,128)(2,1)S(1)}, u32[]{:S(2)}, u32[]{:S(2)}) collective-permute-start(bf16[48,64,128]{2,1,0:T(8,128)(2,1)S(1)} %bitcast.6), channel_id=1, source_target_pairs={{1,0},{2,1},{3,2},{4,3},{5,4},{6,5},{7,6},{8,7},{9,8},{10,9},{11,1... | collective-permute-start | bytes 2359304 | tf_op jit(solution)/shard_map/ppermute | solution.py:241
  30.1 0.0 collective-permute-done.1
  30.1 7.2 %all-to-all-start.1 = ((bf16[16,3,40,128]{3,2,1,0:T(8,128)(2,1)}), bf16[16,3,40,128]{3,2,1,0:T(8,128)(2,1)S(1)}, u32[]{:S(2)}, u32[]{:S(2)}) async-start(bf16[16,3,40,128]{3,2,1,0:T(8,128)(2,1)} %collective-permute-done.1), calls=%async_computation.1 | async-start | bytes 983040 | tf_op jit(solution)/shard_map/all_to_all | solution.py:245
  37.3 0.0 copy-done
  37.3 7.1 %near_pairs.1 = (f32[6144,128]{1,0:T(8,128)}, f32[8200,128]{1,0:T(8,128)}) custom-call(s32[3136]{0:T(1024)} %get-tuple-element.16.job_ref, bf16[48,64,128]{2,1,0:T(8,128)(2,1)} %bitcast.7, bf16[512,1024]{1,0:T(8,128)(2,1)} %constant.15.clone.fwd_ref), custom_call_target="tpu_custom_call" | custom-call | tf_op jit(solution)/shard_map/near_pairs/pallas_call | solution.py:201
  44.4 4.8 %all-to-all-done.1 = bf16[16,3,40,128]{3,2,1,0:T(8,128)(2,1)S(1)} async-done(((bf16[16,3,40,128]{3,2,1,0:T(8,128)(2,1)}), bf16[16,3,40,128]{3,2,1,0:T(8,128)(2,1)S(1)}, u32[]{:S(2)}, u32[]{:S(2)}) %all-to-all-start.1) | async-done | bytes 491552 | tf_op jit(solution)/shard_map/all_to_all | solution.py:245
  49.2 0.0 copy-start.1
  49.2 0.0 collective-permute-done.h1_ref
  49.2 0.0 copy-start.2
  49.2 0.8 %copy-done.1 = bf16[16,3,40,128]{3,2,1,0:T(8,128)(2,1)} copy-done((bf16[16,3,40,128]{3,2,1,0:T(8,128)(2,1)}, bf16[16,3,40,128]{3,2,1,0:T(8,128)(2,1)S(1)}, u32[]{:S(2)}) %copy-start.1) | copy-done | bytes 491544
  50.0 0.3 copy-done.2
  50.3 11.2 %far_pairs.1 = f32[1024,512]{1,0:T(8,128)} custom-call(s32[3136]{0:T(1024)} %get-tuple-element.14.job_ref, bf16[48,64,128]{2,1,0:T(8,128)(2,1)} %copy-done.2, bf16[48,40,128]{2,1,0:T(8,128)(2,1)} %bitcast.8, f32[6144,128]{1,0:T(8,128)} %get-tuple-element.17.spec_in, f32[8200,128]{1,0:T(8,128)} %get-tuple-element.18.cross_in, ...), custom_call_target="tpu_custom_call" | custom-call | tf_op jit(solution)/shard_map/far_pairs/pallas_call | solution.py:219
Async XLA Ops:
  2.1 26.1 %all-to-all-start = ((bf16[16,3,64,128]{3,2,1,0:T(8,128)(2,1)}), bf16[16,3,64,128]{3,2,1,0:T(8,128)(2,1)S(1)}, u32[]{:S(2)}, u32[]{:S(2)}) async-start(bf16[16,3,64,128]{3,2,1,0:T(8,128)(2,1)} %bitcast.5), calls=%async_computation | async-start | bytes 1572864 | tf_op jit(solution)/shard_map/all_to_all | solution.py:245
  10.2 19.8 %collective-permute-start.1 = (bf16[16,3,40,128]{3,2,1,0:T(8,128)(2,1)S(1)}, bf16[16,3,40,128]{3,2,1,0:T(8,128)(2,1)}, u32[]{:S(2)}, u32[]{:S(2)}) collective-permute-start(bf16[16,3,40,128]{3,2,1,0:T(8,128)(2,1)S(1)} %slice.4), channel_id=1, source_target_pairs={{2,0},{3,1},{4,2},{5,3},{6,4},{7,5},{8,6},{9,7},{10,8},{11,9},{12,... | collective-permute-start | bytes 1474568 | tf_op jit(solution)/shard_map/ppermute | solution.py:241
  28.1 9.2 %copy-start = (bf16[16,3,64,128]{3,2,1,0:T(8,128)(2,1)}, bf16[16,3,64,128]{3,2,1,0:T(8,128)(2,1)S(1)}, u32[]{:S(2)}) copy-start(bf16[16,3,64,128]{3,2,1,0:T(8,128)(2,1)S(1)} %all-to-all-done) | copy-start | bytes 2359300
  28.1 21.0 %collective-permute-start = (bf16[48,64,128]{2,1,0:T(8,128)(2,1)S(1)}, bf16[48,64,128]{2,1,0:T(8,128)(2,1)S(1)}, u32[]{:S(2)}, u32[]{:S(2)}) collective-permute-start(bf16[48,64,128]{2,1,0:T(8,128)(2,1)S(1)} %bitcast.6), channel_id=1, source_target_pairs={{1,0},{2,1},{3,2},{4,3},{5,4},{6,5},{7,6},{8,7},{9,8},{10,9},{11,1... | collective-permute-start | bytes 2359304 | tf_op jit(solution)/shard_map/ppermute | solution.py:241
  30.1 19.1 %all-to-all-start.1 = ((bf16[16,3,40,128]{3,2,1,0:T(8,128)(2,1)}), bf16[16,3,40,128]{3,2,1,0:T(8,128)(2,1)S(1)}, u32[]{:S(2)}, u32[]{:S(2)}) async-start(bf16[16,3,40,128]{3,2,1,0:T(8,128)(2,1)} %collective-permute-done.1), calls=%async_computation.1 | async-start | bytes 983040 | tf_op jit(solution)/shard_map/all_to_all | solution.py:245
  49.2 0.8 %copy-start.1 = (bf16[16,3,40,128]{3,2,1,0:T(8,128)(2,1)}, bf16[16,3,40,128]{3,2,1,0:T(8,128)(2,1)S(1)}, u32[]{:S(2)}) copy-start(bf16[16,3,40,128]{3,2,1,0:T(8,128)(2,1)S(1)} %all-to-all-done.1) | copy-start | bytes 1474564
  49.2 1.1 %copy-start.2 = (bf16[48,64,128]{2,1,0:T(8,128)(2,1)}, bf16[48,64,128]{2,1,0:T(8,128)(2,1)S(1)}, u32[]{:S(2)}) copy-start(bf16[48,64,128]{2,1,0:T(8,128)(2,1)S(1)} %collective-permute-done.h1_ref) | copy-start | bytes 2359300

commit v3 on v2

--- a/solution.py
+++ b/solution.py
@@ -74,15 +74,17 @@
     lax.fori_loop(0, total, whiten, 0, unroll=4)
 
 
-def pair_products(job_ref, left_spec, right_spec, cross):
+def pair_products(order_ref, count, pairs_ref, offset, shift, limit, left_spec, right_spec, cross):
+    last = CAP - 1
     low_half = lax.broadcasted_iota(jnp.int32, (8, TILE), 0) < QUADS
 
     def step(n, carry):
         for t in range(UNROLL):
-            slot = n * UNROLL + t
-            i = pl.multiple_of(job_ref[slot], 8)
-            j = pl.multiple_of(job_ref[JOBS + slot], 8)
-            row = pl.multiple_of(job_ref[2 * JOBS + slot], 8)
+            p = order_ref[n * UNROLL + t]
+            slot = jnp.minimum(p, last)
+            i = pl.multiple_of((pairs_ref[0, slot] - offset) * ROWS, 8)
+            j = pl.multiple_of(jnp.clip(pairs_ref[1, slot] - (offset + shift), 0, limit) * ROWS, 8)
+            row = pl.multiple_of(p * 8, 8)
             real = imag = None
             for h in range(SEGS // 2):
                 lr = left_spec[pl.ds(i + h * 8, 8), :]
@@ -100,60 +102,65 @@
             cross[pl.ds(row, 8), :] = jnp.where(low_half, real, imag)
         return carry
 
-    lax.fori_loop(0, (job_ref[3 * JOBS] + UNROLL - 1) // UNROLL, step, 0)
+    lax.fori_loop(0, (count + UNROLL - 1) // UNROLL, step, 0)
 
 
 def order_kernel(pairs_ref, live_ref, offset_ref, near_ref, far_ref):
-    offset = offset_ref[0]
+    bound = offset_ref[0] + OWN
     live = live_ref[0]
 
-    def step(p, carry):
+    def step(n, carry):
         near, far = carry
-        i = (pairs_ref[0, p] - offset) * ROWS
-        j = (pairs_ref[1, p] - offset) * ROWS
-        inside = (j < OWN * ROWS).astype(jnp.int32)
-        active = (p < live).astype(jnp.int32)
-        near_ref[near] = i
-        near_ref[JOBS + near] = jnp.minimum(j, (OWN - 1) * ROWS)
-        near_ref[2 * JOBS + near] = p * 8
-        far_ref[far] = i
-        far_ref[JOBS + far] = jnp.maximum(j - OWN * ROWS, 0)
-        far_ref[2 * JOBS + far] = p * 8
-        near = near + active * inside
-        return near, far + active - active * inside
-
-    near, far = lax.fori_loop(0, CAP, step, (jnp.int32(0), jnp.int32(0)), unroll=8)
+        for t in range(UNROLL):
+            p = n * UNROLL + t
+            inside = (pairs_ref[1, p] < bound).astype(jnp.int32)
+            near_ref[near] = p
+            far_ref[far] = p
+            near = near + inside
+            far = far + 1 - inside
+        return near, far
+
+    blocks = live // UNROLL
+    near, far = lax.fori_loop(0, blocks, step, (jnp.int32(0), jnp.int32(0)))
+
+    def single(p, carry):
+        near, far = carry
+        inside = (pairs_ref[1, p] < bound).astype(jnp.int32)
+        near_ref[near] = p
+        far_ref[far] = p
+        return near + inside, far + 1 - inside
+
+    near, far = lax.fori_loop(blocks * UNROLL, live, single, (near, far))
     for ref, count in ((near_ref, near), (far_ref, far)):
         for t in range(UNROLL):
-            ref[count + t] = 0
-            ref[JOBS + count + t] = 0
-            ref[2 * JOBS + count + t] = CAP * 8
-        ref[3 * JOBS] = count
-        ref[3 * JOBS + 1] = live
-
-
-def near_kernel(job_ref, own_ref, fwd_ref, spec_out, cross_out, scaled, loose, spec, cross, sems):
+            ref[count + t] = CAP
+        ref[JOBS] = count
+        ref[JOBS + 1] = live
+        ref[JOBS + 2] = offset_ref[0]
+
+
+def near_kernel(order_ref, pairs_ref, own_ref, fwd_ref, kept, scaled, loose, spec, cross, sems):
     spectra([own_ref], fwd_ref, scaled, loose, spec)
-    spec_copy = pltpu.make_async_copy(spec, spec_out, sems.at[0])
+    spec_copy = pltpu.make_async_copy(spec, kept.at[pl.ds(0, OWN * ROWS), :], sems.at[0])
     spec_copy.start()
-    pair_products(job_ref, spec, spec, cross)
-    cross_copy = pltpu.make_async_copy(cross, cross_out, sems.at[1])
+    pair_products(order_ref, order_ref[JOBS], pairs_ref, order_ref[JOBS + 2], 0, OWN - 1, spec, spec, cross)
+    cross_copy = pltpu.make_async_copy(cross, kept.at[pl.ds(OWN * ROWS, CROSS[0]), :], sems.at[1])
     cross_copy.start()
     spec_copy.wait()
     cross_copy.wait()
 
 
-def far_kernel(job_ref, h1_ref, h2_ref, spec_in, cross_in, fwd_ref, inv_ref, out_ref,
+def far_kernel(order_ref, pairs_ref, h1_ref, h2_ref, kept, fwd_ref, inv_ref, out_ref,
                scaled, loose, halo, spec, cross, stacks, sems):
-    spec_copy = pltpu.make_async_copy(spec_in, spec, sems.at[0])
-    cross_copy = pltpu.make_async_copy(cross_in, cross, sems.at[1])
+    spec_copy = pltpu.make_async_copy(kept.at[pl.ds(0, OWN * ROWS), :], spec, sems.at[0])
+    cross_copy = pltpu.make_async_copy(kept.at[pl.ds(OWN * ROWS, CROSS[0]), :], cross, sems.at[1])
     spec_copy.start()
     cross_copy.start()
     spectra([h1_ref, h2_ref], fwd_ref, scaled, loose, halo)
     spec_copy.wait()
     cross_copy.wait()
-    pair_products(job_ref, spec, halo, cross)
-    live = job_ref[3 * JOBS + 1]
+    pair_products(order_ref, order_ref[JOBS], pairs_ref, order_ref[JOBS + 2], OWN, HALO - 1, spec, halo, cross)
+    live = order_ref[JOBS + 1]
     copies = []
     for b in range(CAP // BLOCK):
         rows = pl.ds(b * BLOCK, BLOCK)
@@ -190,19 +197,19 @@
 def order_pairs(pair_list, live, offset):
     return pl.pallas_call(
         order_kernel,
-        out_shape=(ints(3 * JOBS + 16), ints(3 * JOBS + 16)),
+        out_shape=(ints(JOBS + 16), ints(JOBS + 16)),
         in_specs=[SMEM] * 3,
         out_specs=(SMEM,) * 2,
         name="order_pairs",
     )(pair_list, live, offset)
 
 
-def near_pairs(jobs, own, fwd):
+def near_pairs(order, pair_list, own, fwd):
     return pl.pallas_call(
         near_kernel,
-        out_shape=(floats(OWN * ROWS, TILE), floats(*CROSS)),
-        in_specs=[SMEM, VMEM, VMEM],
-        out_specs=(HBM,) * 2,
+        out_shape=floats(OWN * ROWS + CROSS[0], TILE),
+        in_specs=[SMEM, SMEM, VMEM, VMEM],
+        out_specs=HBM,
         scratch_shapes=[
             pltpu.VMEM((SEGS * OWN, SEG), jnp.bfloat16),
             pltpu.VMEM((OWN * PITCH + 8, TILE), jnp.float32),
@@ -210,16 +217,16 @@
             pltpu.VMEM(CROSS, jnp.float32),
             pltpu.SemaphoreType.DMA((2,)),
         ],
-        compiler_params=pltpu.CompilerParams(vmem_limit_bytes=60 << 20),
+        compiler_params=pltpu.CompilerParams(vmem_limit_bytes=50 << 20),
         name="near_pairs",
-    )(jobs, own, fwd)
-
-
-def far_pairs(jobs, h1, h2, spec, cross, fwd, inv):
+    )(order, pair_list, own, fwd)
+
+
+def far_pairs(order, pair_list, h1, h2, kept, fwd, inv):
     return pl.pallas_call(
         far_kernel,
         out_shape=floats(CAP, SEG),
-        in_specs=[SMEM, VMEM, VMEM, HBM, HBM, VMEM, VMEM],
+        in_specs=[SMEM, SMEM, VMEM, VMEM, HBM, VMEM, VMEM],
         out_specs=HBM,
         scratch_shapes=[
             pltpu.VMEM((SEGS * HALO, SEG), jnp.bfloat16),
@@ -230,9 +237,36 @@
             pltpu.VMEM((CAP, SEG), jnp.float32),
             pltpu.SemaphoreType.DMA((2 + CAP // BLOCK,)),
         ],
-        compiler_params=pltpu.CompilerParams(vmem_limit_bytes=60 << 20),
+        compiler_params=pltpu.CompilerParams(vmem_limit_bytes=50 << 20),
         name="far_pairs",
-    )(jobs, h1, h2, spec, cross, fwd, inv)
+    )(order, pair_list, h1, h2, kept, fwd, inv)
+
+
+def turn_kernel(panels, part, whole, sems):
+    copies = []
+    for turned in (part, whole):
+        count = turned.shape[2]
+        for a in range(panels.shape[0]):
+            source = panels.at[a, :, pl.ds(0, count), :]
+            copies.append(pltpu.make_async_copy(source, turned.at[:, a], sems.at[len(copies)]))
+    for copy in copies:
+        copy.start()
+    for copy in copies:
+        copy.wait()
+
+
+def turn(panels):
+    tiles, sections, _, width = panels.shape
+    return pl.pallas_call(
+        turn_kernel,
+        out_shape=[
+            jax.ShapeDtypeStruct((sections, tiles, count, width), panels.dtype) for count in (REST, OWN)],
+        in_specs=[HBM],
+        out_specs=[HBM] * 2,
+        scratch_shapes=[pltpu.SemaphoreType.DMA((2 * tiles,))],
+        compiler_params=pltpu.CompilerParams(vmem_limit_bytes=60<<20),
+        name="turn",
+    )(panels)
 
 
 def from_ahead(block, axis, distance):
@@ -250,14 +284,14 @@
     fwd, inv = (jnp.asarray(table) for table in tables())
     offset = (lax.axis_index("tm") * lax.axis_size("pairs") + lax.axis_index("pairs")) * OWN
     near, far = order_pairs(pair_list, pair_count, offset.astype(jnp.int32)[None])
-    turned = jnp.transpose(panels, (1, 0, 2, 3))
-    h2_turned = from_ahead(turned[:, :, :REST], "pairs", 2)
-    own = by_section(turned)
+    part, whole = turn(panels)
+    h2_turned = from_ahead(part, "pairs", 2)
+    own = by_section(whole)
+    h2 = by_section(h2_turned)
     own, near, far = lax.optimization_barrier((own, near, far))
     h1 = from_ahead(own, "pairs", 1)
-    h2 = by_section(h2_turned)
-    spec, cross = near_pairs(near, own, fwd)
-    return far_pairs(far, h1, h2, spec, cross, fwd, inv)
+    kept = near_pairs(near, pair_list, own, fwd)
+    return far_pairs(far, pair_list, h1, h2, kept, fwd, inv)
 
 
 def solution(mesh):

time: 61.8 us -> 94.7 us (1.53)
  the two profiles are of different devices: /device:TPU:224 before, /device:TPU:96 now
where the time goes in v3:
time: 94.7 us; the launch traced here: 93.7 us
  Pallas kernels  66.2 us (70%)
  starting transfers between devices  17.9 us (19%)
  waiting for transfers between devices  6.21 us (7%)
  local copies, waits for them, and re-layouts  2.63 us (3%)
    pallas_call x1, Pallas kernels, turn(): pl.pallas_call(turn_kernel, out_shape=[jax.ShapeDtypeStruct((sections, ti...  39.9 us
    all_to_all x2, starting transfers between devices, by_section(): rows = lax.all_to_all(block, 'tm', split_axis=0, concat_axis=0, tiled=True)  14 us
    pallas_call x1, Pallas kernels, far_pairs(): pl.pallas_call(far_kernel, out_shape=floats(CAP, SEG), in_specs=[SMEM, SM...  13.6 us
    pallas_call x1, Pallas kernels, near_pairs(): pl.pallas_call(near_kernel, out_shape=floats(OWN * ROWS + CROSS[0], TILE)...  6.88 us
    all_to_all x2, waiting for transfers between devices, by_section(): rows = lax.all_to_all(block, 'tm', split_axis=0, concat_axis=0, tiled=True)  6.21 us
    pallas_call x1, Pallas kernels, order_pairs(): pl.pallas_call(order_kernel, out_shape=(ints(JOBS + 16), ints(JOBS + 16))...  5.86 us
    ppermute x2, starting transfers between devices, from_ahead(): return lax.ppermute(block, axis, route)  3.93 us
    unnamed x14, local copies, waits for them, and re-layouts  2.63 us
  transfers between devices with their start and end apart: 4, of which 2 were waited for; matrix products, arithmetic and copies ran while one was open for 0% of the time, Pallas kernels for 14%

profile of v3, /device:TPU:96, one launch (start us, length us, event | category | flops | bytes accessed | tf_op | source)
XLA Modules:
  0.0 93.7 jit_solution(14284730406771270383)
XLA Ops:
  0.0 0.0 copy-start.1
  0.0 0.0 copy-start.2
  0.0 0.0 copy-start.4
  0.0 39.9 %turn.1 = (bf16[16,3,40,128]{3,2,1,0:T(8,128)(2,1)}, bf16[16,3,64,128]{3,2,1,0:T(8,128)(2,1)}) custom-call(bf16[3,16,64,128]{3,2,1,0:T(8,128)(2,1)} %panels.1), custom_call_target="tpu_custom_call" | custom-call | tf_op jit(solution)/shard_map/turn/pallas_call | solution.py:260
  39.9 7.0 %all-to-all-start = ((bf16[16,3,64,128]{3,2,1,0:T(8,128)(2,1)}), bf16[16,3,64,128]{3,2,1,0:T(8,128)(2,1)S(1)}, u32[]{:S(2)}, u32[]{:S(2)}) async-start(bf16[16,3,64,128]{3,2,1,0:T(8,128)(2,1)} %get-tuple-element.12), calls=%async_computation | async-start | bytes 1572864 | tf_op jit(solution)/shard_map/all_to_all | solution.py:279
  46.9 2.0 %collective-permute-start.1 = (bf16[16,3,40,128]{3,2,1,0:T(8,128)(2,1)}, bf16[16,3,40,128]{3,2,1,0:T(8,128)(2,1)}, u32[]{:S(2)}, u32[]{:S(2)}) collective-permute-start(bf16[16,3,40,128]{3,2,1,0:T(8,128)(2,1)} %get-tuple-element.17), channel_id=1, source_target_pairs={{2,0},{3,1},{4,2},{5,3},{6,4},{7,5},{8,6},{9,7},{10,8},{11,9},{12,... | collective-permute-start | bytes 1474568 | tf_op jit(solution)/shard_map/ppermute | solution.py:275
  49.6 5.9 %order_pairs.1 = (s32[1056]{0:T(1024)}, s32[1056]{0:T(1024)}) custom-call(s32[2,1024]{1,0:T(2,128)} %pairs_ref.5, s32[1]{0:T(128)S(6)} %copy.6.live_ref, s32[1]{0:T(128)} %bitcast.1.offset_ref), custom_call_target="tpu_custom_call" | custom-call | tf_op jit(solution)/shard_map/order_pairs/pallas_call | solution.py:198
  55.5 0.0 copy-start.5
  55.5 5.8 %all-to-all-done = bf16[16,3,64,128]{3,2,1,0:T(8,128)(2,1)S(1)} async-done(((bf16[16,3,64,128]{3,2,1,0:T(8,128)(2,1)}), bf16[16,3,64,128]{3,2,1,0:T(8,128)(2,1)S(1)}, u32[]{:S(2)}, u32[]{:S(2)}) %all-to-all-start) | async-done | bytes 786464 | tf_op jit(solution)/shard_map/all_to_all | solution.py:279
  61.3 1.9 %collective-permute-start = (bf16[48,64,128]{2,1,0:T(8,128)(2,1)S(1)}, bf16[48,64,128]{2,1,0:T(8,128)(2,1)}, u32[]{:S(2)}, u32[]{:S(2)}) collective-permute-start(bf16[48,64,128]{2,1,0:T(8,128)(2,1)S(1)} %bitcast.3), channel_id=1, source_target_pairs={{1,0},{2,1},{3,2},{4,3},{5,4},{6,5},{7,6},{8,7},{9,8},{10,9},{11,1... | collective-permute-start | bytes 2359304 | tf_op jit(solution)/shard_map/ppermute | solution.py:275
  63.2 0.0 collective-permute-done.1
  63.2 6.9 %all-to-all-start.1 = ((bf16[16,3,40,128]{3,2,1,0:T(8,128)(2,1)}), bf16[16,3,40,128]{3,2,1,0:T(8,128)(2,1)S(1)}, u32[]{:S(2)}, u32[]{:S(2)}) async-start(bf16[16,3,40,128]{3,2,1,0:T(8,128)(2,1)} %collective-permute-done.1), calls=%async_computation.1 | async-start | bytes 983040 | tf_op jit(solution)/shard_map/all_to_all | solution.py:279
  70.2 0.0 copy-start
  70.2 1.2 %copy-done = bf16[512,1024]{1,0:T(8,128)(2,1)S(1)} copy-done((bf16[512,1024]{1,0:T(8,128)(2,1)S(1)}, bf16[512,1024]{1,0:T(8,128)(2,1)}, u32[]{:S(2)}) %copy-start) | copy-done | bytes 1048600
  71.4 0.0 copy-start.3
  71.4 0.7 copy-done.3
  72.1 0.0 copy-start.6
  72.1 0.7 copy-done.6
  72.8 6.9 %near_pairs.1.kept = f32[14344,128]{1,0:T(8,128)} custom-call(s32[1056]{0:T(1024)S(1)} %copy-done.6, s32[2,1024]{1,0:T(2,128)S(1)} %copy-done.3, bf16[48,64,128]{2,1,0:T(8,128)(2,1)S(1)} %bitcast.4, bf16[512,1024]{1,0:T(8,128)(2,1)S(1)} %copy-done), custom_call_target="tpu_custom_call" | custom-call | tf_op jit(solution)/shard_map/near_pairs/pallas_call | solution.py:208
  79.7 0.4 all-to-all-done.1
  80.1 0.0 collective-permute-done.h1_ref
  80.1 0.0 copy-done.1
  80.1 0.0 copy-done.2
  80.1 0.0 copy-done.4
  80.1 0.0 copy-done.5
  80.1 13.6 %far_pairs.1 = f32[1024,512]{1,0:T(8,128)} custom-call(s32[1056]{0:T(1024)S(1)} %copy-done.5, s32[2,1024]{1,0:T(2,128)S(1)} %copy-done.4, bf16[48,64,128]{2,1,0:T(8,128)(2,1)} %collective-permute-done.h1_ref, bf16[48,40,128]{2,1,0:T(8,128)(2,1)S(1)} %bitcast.5, f32[14344,128]{1,0:T(8,128)} %near_pairs.1.kept, bf16[512,1024]{1,0:T(8,128)(2,1)S(1)} %copy-done.1, ...), custom_call_target="tpu_custom_call" | custom-call | tf_op jit(solution)/shard_map/far_pairs/pallas_call | solution.py:226
Async XLA Ops:
  0.0 80.1 %copy-start.1 = (bf16[512,1024]{1,0:T(8,128)(2,1)S(1)}, bf16[512,1024]{1,0:T(8,128)(2,1)}, u32[]{:S(2)}) copy-start(bf16[512,1024]{1,0:T(8,128)(2,1)} %constant.15.clone.fwd_ref) | copy-start | bytes 3145732
  0.0 80.1 %copy-start.2 = (bf16[1024,512]{1,0:T(8,128)(2,1)S(1)}, bf16[1024,512]{1,0:T(8,128)(2,1)}, u32[]{:S(2)}) copy-start(bf16[1024,512]{1,0:T(8,128)(2,1)} %constant.16.clone.inv_ref) | copy-start | bytes 3145732
  0.0 80.1 %copy-start.4 = (s32[2,1024]{1,0:T(2,128)S(1)}, s32[2,1024]{1,0:T(2,128)}, u32[]{:S(2)}) copy-start(s32[2,1024]{1,0:T(2,128)} %pairs_ref.5) | copy-start | bytes 24580
  39.9 21.4 %all-to-all-start = ((bf16[16,3,64,128]{3,2,1,0:T(8,128)(2,1)}), bf16[16,3,64,128]{3,2,1,0:T(8,128)(2,1)S(1)}, u32[]{:S(2)}, u32[]{:S(2)}) async-start(bf16[16,3,64,128]{3,2,1,0:T(8,128)(2,1)} %get-tuple-element.12), calls=%async_computation | async-start | bytes 1572864 | tf_op jit(solution)/shard_map/all_to_all | solution.py:279
  46.9 16.3 %collective-permute-start.1 = (bf16[16,3,40,128]{3,2,1,0:T(8,128)(2,1)}, bf16[16,3,40,128]{3,2,1,0:T(8,128)(2,1)}, u32[]{:S(2)}, u32[]{:S(2)}) collective-permute-start(bf16[16,3,40,128]{3,2,1,0:T(8,128)(2,1)} %get-tuple-element.17), channel_id=1, source_target_pairs={{2,0},{3,1},{4,2},{5,3},{6,4},{7,5},{8,6},{9,7},{10,8},{11,9},{12,... | collective-permute-start | bytes 1474568 | tf_op jit(solution)/shard_map/ppermute | solution.py:275
  55.5 24.6 %copy-start.5 = (s32[1056]{0:T(1024)S(1)}, s32[1056]{0:T(1024)}, u32[]{:S(2)}) copy-start(s32[1056]{0:T(1024)} %get-tuple-element.15.order_ref) | copy-start | bytes 12676
  61.3 18.8 %collective-permute-start = (bf16[48,64,128]{2,1,0:T(8,128)(2,1)S(1)}, bf16[48,64,128]{2,1,0:T(8,128)(2,1)}, u32[]{:S(2)}, u32[]{:S(2)}) collective-permute-start(bf16[48,64,128]{2,1,0:T(8,128)(2,1)S(1)} %bitcast.3), channel_id=1, source_target_pairs={{1,0},{2,1},{3,2},{4,3},{5,4},{6,5},{7,6},{8,7},{9,8},{10,9},{11,1... | collective-permute-start | bytes 2359304 | tf_op jit(solution)/shard_map/ppermute | solution.py:275
  63.2 16.9 %all-to-all-start.1 = ((bf16[16,3,40,128]{3,2,1,0:T(8,128)(2,1)}), bf16[16,3,40,128]{3,2,1,0:T(8,128)(2,1)S(1)}, u32[]{:S(2)}, u32[]{:S(2)}) async-start(bf16[16,3,40,128]{3,2,1,0:T(8,128)(2,1)} %collective-permute-done.1), calls=%async_computation.1 | async-start | bytes 983040 | tf_op jit(solution)/shard_map/all_to_all | solution.py:279
  70.2 1.2 %copy-start = (bf16[512,1024]{1,0:T(8,128)(2,1)S(1)}, bf16[512,1024]{1,0:T(8,128)(2,1)}, u32[]{:S(2)}) copy-start(bf16[512,1024]{1,0:T(8,128)(2,1)} %constant.15.clone.fwd_ref) | copy-start | bytes 3145732
  71.4 0.7 copy-start.3
  72.1 0.7 copy-start.6
